TPU v7x, 256 devices: a whole 4x4x8 slice. The times are simulated.
256 devices in a mesh: cells: 16 (over z_hi, x, core), modes: 16 (over y, z_lo).
Axes of the slice: x: 4, y: 4, z: 8 (z_hi: 2, z_lo: 4; z = z_hi * 4 + z_lo), core: 2. Of those that a mesh axis runs over, the one named last changes fastest.
Arguments:
- hermite_coefficient_array: float32 [32, 64, 32, 2048], P('cells', None, None, 'modes'), may hold values from -6 to 6
- encounter_kernel_array: bfloat16 [14400, 120], replicated, may hold values from -0.046875 to 0.046875
- obstacle_indicator: int32 [32, 64, 32], P('cells'), may hold values 0 or 1
Outputs:
- moments_next: float32 [32, 64, 32, 2048], P('cells', None, None, 'modes')
All inputs are finite; a program needn't handle non-finite values. No bound on the sum of `obstacle_indicator` on one device may be relied on, other than what follows from the above.
Results may differ from a plain program's by a relative error of at most 0.0003.
Values sent between devices are 32-bit elements; how exact they have to be, the bound alone decides.
No kernel may reach another device: no remote copies, remote signals or barrier semaphores. Data moves between devices by JAX's collectives and lax.ppermute only.
A program may use at most 64 MiB of HBM per device.

v0:
```python
import math
import jax
import jax.numpy as jnp
from jax import lax
from jax.sharding import PartitionSpec as P

MA = 16
MB = 16
MC = 8
LDEG = 7
BASIS_SIZE = 120
MODES = 2048
CFL = 0.04
DTC = 0.2
PRECISE = lax.Precision.HIGHEST


def passed_along(shard, axis, by):
    length = lax.axis_size(axis)
    pairs = [(i, i + by) for i in range(length) if 0 <= i + by < length]
    return lax.ppermute(shard, axis, pairs)


def extended(cells, sides, width):
    for axis, dim in sides:
        count = lax.axis_size(axis)
        head = lax.slice_in_dim(cells, 0, width, axis=dim)
        tail = lax.slice_in_dim(cells, cells.shape[dim] - width, cells.shape[dim], axis=dim)
        cells = jnp.concatenate(
            [
                lax.ppermute(tail, axis, [(i, (i + 1) % count) for i in range(count)]),
                cells,
                lax.ppermute(head, axis, [((i + 1) % count, i) for i in range(count)]),
            ],
            axis=dim,
        )
    return cells


def digits(mode_index):
    digit_a = mode_index // (MB * MC)
    digit_b = mode_index // MC % MB
    digit_c = mode_index % MC
    return (digit_a, digit_b, digit_c)


def ladder(source, target, same_rest):
    level = target.astype(jnp.float32)
    down_term = jnp.where(same_rest & (source == target - 1), jnp.sqrt(level), 0.0)
    up_term = jnp.where(same_rest & (source == target + 1), jnp.sqrt(level + 1.0), 0.0)
    return down_term + up_term


def coupling(first_mode, local_modes):
    mode_index = first_mode + jnp.arange(local_modes, dtype=jnp.int32)
    source_a, source_b, source_c = digits(mode_index[:, None])
    target_a, target_b, target_c = digits(mode_index[None, :])
    same_a = source_a == target_a
    same_b = source_b == target_b
    same_c = source_c == target_c
    x_matrix = ladder(source_a, target_a, same_b & same_c)
    y_matrix = ladder(source_b, target_b, same_a & same_c)
    z_matrix = ladder(source_c, target_c, same_a & same_b)
    return (x_matrix, jnp.concatenate([y_matrix, z_matrix], 0))


def body(hermite_coefficient_array, encounter_kernel_array, obstacle_indicator):
    plane_count, rows_y, rows_z, local_modes = hermite_coefficient_array.shape
    block_size = MB * MC
    speed_x = 2.0 * math.sqrt(MA)
    speed_y = 2.0 * math.sqrt(MB)
    speed_z = 2.0 * math.sqrt(MC)
    all_index = jnp.arange(MODES, dtype=jnp.int32)
    all_a, all_b, all_c = digits(all_index)
    low_flags = (all_a + all_b + all_c <= LDEG).astype(jnp.int32)
    rank_all = jnp.cumsum(low_flags) - 1
    targets = jnp.arange(BASIS_SIZE, dtype=jnp.int32)
    first_mode = lax.axis_index("modes") * local_modes
    first_a = (first_mode // block_size).astype(jnp.float32)
    last_a = first_a + float(local_modes // block_size - 1)
    x_matrix, yz_matrix = coupling(first_mode, local_modes)
    full_matrix = jnp.concatenate([x_matrix, yz_matrix], 0)

    def across(first_axis_gradient):
        from_lower = passed_along(first_axis_gradient, "modes", 1)
        from_upper = passed_along(first_axis_gradient, "modes", -1)
        lower_term = jnp.sqrt(first_a) * from_lower
        upper_term = jnp.sqrt(last_a + 1.0) * from_upper
        return lower_term + upper_term

    def substep(center, behind, beyond, solid):
        first_axis_gradient = beyond - behind
        lap_x = beyond - 2.0 * center + behind
        next_y = jnp.roll(center, -1, 1)
        prev_y = jnp.roll(center, 1, 1)
        next_z = jnp.roll(center, -1, 2)
        prev_z = jnp.roll(center, 1, 2)
        diff_y = next_y - prev_y
        lap_y = next_y - 2.0 * center + prev_y
        diff_z = next_z - prev_z
        lap_z = next_z - 2.0 * center + prev_z
        flux = jnp.dot(
            jnp.concatenate([first_axis_gradient, diff_y, diff_z], -1),
            full_matrix,
            precision=PRECISE,
            preferred_element_type=jnp.float32,
        )
        flux = flux + across(first_axis_gradient)
        update = center + CFL * (
            -0.5 * flux + 0.5 * (speed_x * lap_x + speed_y * lap_y + speed_z * lap_z)
        )
        return jnp.where(solid[..., None] != 0, center, update)

    def widen(field):
        return extended(field, (("cells", 0),), 1)

    padded = widen(hermite_coefficient_array)
    middle = substep(hermite_coefficient_array, padded[:-2], padded[2:], obstacle_indicator)
    padded = widen(middle)
    transported = substep(middle, padded[:-2], padded[2:], obstacle_indicator)
    cell_count = plane_count * rows_y * rows_z
    rows = transported.reshape(cell_count, local_modes)
    local_flags = lax.dynamic_slice_in_dim(low_flags, first_mode, local_modes)
    local_rank = lax.dynamic_slice_in_dim(rank_all, first_mode, local_modes)
    selector = ((local_flags[:, None] == 1) & (local_rank[:, None] == targets[None, :])).astype(
        jnp.float32
    )
    share_rows = cell_count // lax.axis_size("modes")
    low = lax.psum_scatter(
        jnp.dot(rows, selector, precision=PRECISE, preferred_element_type=jnp.float32),
        "modes",
        scatter_dimension=0,
        tiled=True,
    )
    quadratic_factors = (
        (low[:, :, None] * low[:, None, :])
        .reshape(share_rows, BASIS_SIZE * BASIS_SIZE)
        .astype(jnp.bfloat16)
    )
    scattered_state = jnp.dot(
        quadratic_factors, encounter_kernel_array, preferred_element_type=jnp.float32
    )
    lifted = jnp.dot(
        lax.all_gather(scattered_state, "modes", axis=0, tiled=True),
        selector.T,
        precision=PRECISE,
        preferred_element_type=jnp.float32,
    )
    result = rows + DTC * lifted
    return result.reshape(plane_count, rows_y, rows_z, local_modes)


def solution(mesh):
    placed = (P("cells", None, None, "modes"), P(), P("cells", None, None))
    return jax.shard_map(
        body, mesh=mesh, in_specs=placed, out_specs=P("cells", None, None, "modes"), check_vma=False
    )
```

profile of v0, /device:TPU:6, one launch (start us, length us, event | category | flops | bytes accessed | tf_op | source)
XLA Modules:
  0.0 488.2 jit_solution(3035547686091999700)
XLA Ops:
  6.5 3.2 fusion.65
  9.7 1.7 collective-permute-start
  12.4 11.9 %collective-permute-done.1 = f32[1,64,32,128]{3,2,1,0:T(8,128)} collective-permute-done((f32[1,64,32,128]{3,2,1,0:T(8,128)}, f32[1,64,32,128]{3,2,1,0:T(8,128)}, u32[]{:S(2)}, u32[]{:S(2)}) %collective-permute-start.1) | collective-permute-done | bytes 1048608 | tf_op jit(solution)/shard_map/ppermute | solution.py:31
  24.3 2.7 fusion.23
  26.9 1.3 collective-permute-start.3
  28.2 4.7 collective-permute-start.2
  36.3 35.2 %collective-permute-done.3 = f32[2,64,32,128]{3,2,1,0:T(8,128)S(1)} collective-permute-done((f32[2,64,32,128]{3,2,1,0:T(8,128)S(1)}, f32[2,64,32,128]{3,2,1,0:T(8,128)S(1)}, u32[]{:S(2)}, u32[]{:S(2)}) %collective-permute-start.3) | collective-permute-done | bytes 2097184 | tf_op jit(solution)/shard_map/ppermute | solution.py:21
  71.5 1.3 copy-done.8
  73.5 9.4 %add_select_fusion.1 = f32[2,64,32,128]{3,2,1,0:T(8,128)S(1)} fusion(f32[2,64,32,128]{3,2,1,0:T(8,128)S(1)} %copy-done.1, f32[2,64,32,128]{3,2,1,0:T(8,128)} %copy-done.8, f32[2,64,32,128]{3,2,1,0:T(8,128)} %copy-done.9, f32[2,63,32,128]{3,2,1,0:T(8,128)S(1)} %get-tuple-element.20, f32[2,1,32,128]{3,2,1,0:T(8,128)S(1)} %get-tuple-element.22, ...), kind=kOutput, calls=%fused_computation.16 | convolution fusion | flops 2433318912 | bytes 25366536 | tf_op jit(solution)/shard_map/dot_general | solution.py:102
  82.9 1.6 fusion.60
  84.9 59.8 %collective-permute-start.5 = (f32[1,64,32,128]{3,2,1,0:T(8,128)}, f32[1,64,32,128]{3,2,1,0:T(8,128)}, u32[]{:S(2)}, u32[]{:S(2)}) collective-permute-start(f32[1,64,32,128]{3,2,1,0:T(8,128)} %get-tuple-element.13), channel_id=1, source_target_pairs={{0,16},{16,32},{32,48},{48,64},{64,80},{80,96},{96,112},{112,128},... | collective-permute-start | bytes 3145736 | tf_op jit(solution)/shard_map/ppermute | solution.py:31
  147.3 10.0 %collective-permute-done.4 = f32[1,64,32,128]{3,2,1,0:T(8,128)} collective-permute-done((f32[1,64,32,128]{3,2,1,0:T(8,128)}, f32[1,64,32,128]{3,2,1,0:T(8,128)}, u32[]{:S(2)}, u32[]{:S(2)}) %collective-permute-start.4) | collective-permute-done | bytes 1048608 | tf_op jit(solution)/shard_map/ppermute | solution.py:33
  157.3 2.6 fusion.24
  161.3 5.9 %collective-permute-start.6 = (f32[2,64,32,128]{3,2,1,0:T(8,128)S(1)}, f32[2,64,32,128]{3,2,1,0:T(8,128)}, u32[]{:S(2)}, u32[]{:S(2)}) collective-permute-start(f32[2,64,32,128]{3,2,1,0:T(8,128)S(1)} %fusion.24), channel_id=1, source_target_pairs={{0,1},{1,2},{2,3},{3,4},{4,5},{5,6},{6,7},{7,8},{8,9},{9,10},{10,1... | collective-permute-start | bytes 6291464 | tf_op jit(solution)/shard_map/ppermute | solution.py:21
  169.7 52.6 %collective-permute-done.7 = f32[2,64,32,128]{3,2,1,0:T(8,128)S(1)} collective-permute-done((f32[2,64,32,128]{3,2,1,0:T(8,128)S(1)}, f32[2,64,32,128]{3,2,1,0:T(8,128)S(1)}, u32[]{:S(2)}, u32[]{:S(2)}) %collective-permute-start.7) | collective-permute-done | bytes 2097184 | tf_op jit(solution)/shard_map/ppermute | solution.py:21
  222.4 1.3 copy-done.10
  223.7 9.4 %add_select_fusion = f32[2,64,32,128]{3,2,1,0:T(8,128)S(1)} fusion(f32[2,64,32,128]{3,2,1,0:T(8,128)S(1)} %copy-done.3, f32[2,64,32,128]{3,2,1,0:T(8,128)} %copy-done.10, f32[2,64,32,128]{3,2,1,0:T(8,128)} %collective-permute-done.6, f32[2,63,32,128]{3,2,1,0:T(8,128)S(1)} %get-tuple-element.10, f32[2,1,32,128]{3,2,1,0:T(8,128)S(1)} %get-tuple-element.12, ...), kind=kOutput, calls=%fused_computation.15 | convolution fusion | flops 2433318912 | bytes 25366536 | tf_op jit(solution)/shard_map/dot_general | solution.py:102
  233.1 1.3 copy-done.4
  234.4 2.5 fusion.27
  237.0 149.5 %reduce-scatter.2.cloned.1.call-done = f32[256,120]{0,1:T(8,128)} async-done(((f32[4096,120]{0,1:T(8,128)}), f32[256,120]{0,1:T(8,128)}) %reduce-scatter.2.cloned.1.call-update) | async-done | bytes 122896 | tf_op jit(solution)/shard_map/reduce_scatter | solution.py:129
  386.5 3.7 multiply_convert_fusion
  390.3 2.8 fusion.66
  393.1 83.6 %all-gather.2.cloned.1.call-done = f32[4096,120]{1,0:T(8,128)} async-done(((f32[256,120]{1,0:T(8,128)}), f32[4096,120]{1,0:T(8,128)}) %all-gather.2.cloned.1.call-update) | async-done | bytes 1966096 | tf_op jit(solution)/shard_map/all_gather | solution.py:144
  476.6 4.7 fusion.12
  (65 shorter events, 11.7 us)
Async XLA Ops:
  6.5 383.7 %copy-start = (bf16[14400,120]{0,1:T(8,128)(2,1)S(1)}, bf16[14400,120]{0,1:T(8,128)(2,1)}, u32[]{:S(2)}) copy-start(bf16[14400,120]{0,1:T(8,128)(2,1)} %param.4) | copy-start | bytes 10368004
  6.5 5.0 %copy-start.5 = (s32[2,64,32]{1,2,0:T(8,128)S(1)}, s32[2,64,32]{1,2,0:T(8,128)}, u32[]{:S(2)}) copy-start(s32[2,64,32]{1,2,0:T(8,128)} %param.5) | copy-start | bytes 49156
  6.5 380.0 %reduce-scatter.2.cloned.1.call-start = ((), (), s32[]{:S(2)}) async-start(), calls=%async_computation.1 | async-start | bytes 2088960 | tf_op jit(solution)/shard_map/reduce_scatter | solution.py:129
  9.7 14.5 %collective-permute-start.1 = (f32[1,64,32,128]{3,2,1,0:T(8,128)}, f32[1,64,32,128]{3,2,1,0:T(8,128)}, u32[]{:S(2)}, u32[]{:S(2)}) collective-permute-start(f32[1,64,32,128]{3,2,1,0:T(8,128)} %get-tuple-element.23), channel_id=1, source_target_pairs={{0,16},{16,32},{32,48},{48,64},{64,80},{80,96},{96,112},{112,128},... | collective-permute-start | bytes 3145736 | tf_op jit(solution)/shard_map/ppermute | solution.py:31
  9.7 14.5 %collective-permute-start = (f32[1,64,32,128]{3,2,1,0:T(8,128)}, f32[1,64,32,128]{3,2,1,0:T(8,128)}, u32[]{:S(2)}, u32[]{:S(2)}) collective-permute-start(f32[1,64,32,128]{3,2,1,0:T(8,128)} %get-tuple-element.24), channel_id=1, source_target_pairs={{16,0},{32,16},{48,32},{64,48},{80,64},{96,80},{112,96},{128,112},... | collective-permute-start | bytes 3145736 | tf_op jit(solution)/shard_map/ppermute | solution.py:33
  12.4 20.6 %copy-start.1 = (f32[2,64,32,128]{3,2,1,0:T(8,128)S(1)}, f32[2,64,32,128]{3,2,1,0:T(8,128)}, u32[]{:S(2)}) copy-start(f32[2,64,32,128]{3,2,1,0:T(8,128)} %param.3) | copy-start | bytes 6291460
  26.9 44.5 %collective-permute-start.3 = (f32[2,64,32,128]{3,2,1,0:T(8,128)S(1)}, f32[2,64,32,128]{3,2,1,0:T(8,128)S(1)}, u32[]{:S(2)}, u32[]{:S(2)}) collective-permute-start(f32[2,64,32,128]{3,2,1,0:T(8,128)S(1)} %fusion.23), channel_id=1, source_target_pairs={{1,0},{2,1},{3,2},{4,3},{5,4},{6,5},{7,6},{8,7},{9,8},{10,9},{11,1... | collective-permute-start | bytes 6291464 | tf_op jit(solution)/shard_map/ppermute | solution.py:21
  28.2 43.2 %collective-permute-start.2 = (f32[2,64,32,128]{3,2,1,0:T(8,128)S(1)}, f32[2,64,32,128]{3,2,1,0:T(8,128)S(1)}, u32[]{:S(2)}, u32[]{:S(2)}) collective-permute-start(f32[2,64,32,128]{3,2,1,0:T(8,128)S(1)} %fusion.23), channel_id=1, source_target_pairs={{0,1},{1,2},{2,3},{3,4},{4,5},{5,6},{6,7},{7,8},{8,9},{9,10},{10,1... | collective-permute-start | bytes 6291464 | tf_op jit(solution)/shard_map/ppermute | solution.py:21
  34.4 39.1 %copy-start.6 = (pred[2,64,32]{2,1,0:T(8,128)(4,1)S(1)}, pred[2,64,32]{2,1,0:T(8,128)(4,1)}, u32[]{:S(2)}) copy-start(pred[2,64,32]{2,1,0:T(8,128)(4,1)} %copy.7) | copy-start | bytes 12292
  71.4 1.3 copy-start.8
  71.4 2.0 copy-start.9
  82.9 2.0 copy-start.2
  84.9 62.4 %collective-permute-start.5 = (f32[1,64,32,128]{3,2,1,0:T(8,128)}, f32[1,64,32,128]{3,2,1,0:T(8,128)}, u32[]{:S(2)}, u32[]{:S(2)}) collective-permute-start(f32[1,64,32,128]{3,2,1,0:T(8,128)} %get-tuple-element.13), channel_id=1, source_target_pairs={{0,16},{16,32},{32,48},{48,64},{64,80},{80,96},{96,112},{112,128},... | collective-permute-start | bytes 3145736 | tf_op jit(solution)/shard_map/ppermute | solution.py:31
  144.7 12.6 %collective-permute-start.4 = (f32[1,64,32,128]{3,2,1,0:T(8,128)}, f32[1,64,32,128]{3,2,1,0:T(8,128)}, u32[]{:S(2)}, u32[]{:S(2)}) collective-permute-start(f32[1,64,32,128]{3,2,1,0:T(8,128)} %get-tuple-element.14), channel_id=1, source_target_pairs={{16,0},{32,16},{48,32},{64,48},{80,64},{96,80},{112,96},{128,112},... | collective-permute-start | bytes 3145736 | tf_op jit(solution)/shard_map/ppermute | solution.py:33
  146.7 20.6 %copy-start.3 = (f32[2,64,32,128]{3,2,1,0:T(8,128)S(1)}, f32[2,64,32,128]{3,2,1,0:T(8,128)}, u32[]{:S(2)}) copy-start(f32[2,64,32,128]{3,2,1,0:T(8,128)} %copy-done.2) | copy-start | bytes 6291460
  160.0 62.4 %collective-permute-start.7 = (f32[2,64,32,128]{3,2,1,0:T(8,128)S(1)}, f32[2,64,32,128]{3,2,1,0:T(8,128)S(1)}, u32[]{:S(2)}, u32[]{:S(2)}) collective-permute-start(f32[2,64,32,128]{3,2,1,0:T(8,128)S(1)} %fusion.24), channel_id=1, source_target_pairs={{1,0},{2,1},{3,2},{4,3},{5,4},{6,5},{7,6},{8,7},{9,8},{10,9},{11,1... | collective-permute-start | bytes 6291464 | tf_op jit(solution)/shard_map/ppermute | solution.py:21
  161.3 62.4 %collective-permute-start.6 = (f32[2,64,32,128]{3,2,1,0:T(8,128)S(1)}, f32[2,64,32,128]{3,2,1,0:T(8,128)}, u32[]{:S(2)}, u32[]{:S(2)}) collective-permute-start(f32[2,64,32,128]{3,2,1,0:T(8,128)S(1)} %fusion.24), channel_id=1, source_target_pairs={{0,1},{1,2},{2,3},{3,4},{4,5},{5,6},{6,7},{7,8},{8,9},{9,10},{10,1... | collective-permute-start | bytes 6291464 | tf_op jit(solution)/shard_map/ppermute | solution.py:21
  169.2 54.5 %copy-start.7 = (pred[2,64,32]{2,1,0:T(8,128)(4,1)S(1)}, pred[2,64,32]{2,1,0:T(8,128)(4,1)}, u32[]{:S(2)}) copy-start(pred[2,64,32]{2,1,0:T(8,128)(4,1)} %copy.7) | copy-start | bytes 12292
  222.4 1.3 copy-start.10
  233.1 1.3 copy-start.4
  237.0 239.6 %all-gather.2.cloned.1.call-start = ((), (), s32[]{:S(2)}) async-start(), calls=%async_computation.2 | async-start | bytes 2228224 | tf_op jit(solution)/shard_map/all_gather | solution.py:144
Sparse Core Ops, SparseCore 0:
  237.1 149.3 reduce-scatter.1
  393.2 83.3 all-gather.1
where the time goes:
time: 488 us
  waiting for transfers between devices  343 us (70%)
  starting transfers between devices  74.7 us (15%)
  matrix products  28.8 us (6%)
  local copies, waits for them, and re-layouts  14.2 us (3%)
  between operations  13.8 us (3%)
  other arithmetic  13.3 us (3%)
    reduce_scatter x1, waiting for transfers between devices, body(): lax.psum_scatter(jnp.dot(rows, selector, precision=PRECISE, preferred_ele...  149 us
    ppermute x4, waiting for transfers between devices, passed_along(): return lax.ppermute(shard, axis, pairs)  87.8 us
    all_gather x1, waiting for transfers between devices, body(): lax.all_gather(scattered_state, 'modes', axis=0, tiled=True)  83.6 us
    ppermute x2, starting transfers between devices, extended(): lax.ppermute(tail, axis, [(i, (i + 1) % count) for i in range(count)])  59.8 us
    dot_general x2, matrix products, substep(): jnp.dot(jnp.concatenate([first_axis_gradient, diff_y, diff_z], -1), full_...  18.8 us
    ppermute x4, starting transfers between devices, passed_along(): return lax.ppermute(shard, axis, pairs)  13.2 us
    ppermute x2, waiting for transfers between devices, extended(): lax.ppermute(tail, axis, [(i, (i + 1) % count) for i in range(count)])  12.5 us
    ppermute x2, waiting for transfers between devices, extended(): lax.ppermute(head, axis, [((i + 1) % count, i) for i in range(count)])  10 us
  transfers between devices with their start and end apart: 10, of which 7 were waited for; matrix products, arithmetic and copies ran while one was open for 2% of the time, Pallas kernels for 0%

commit v1 on v0

--- a/solution.py
+++ b/solution.py
@@ -1,3 +1,4 @@
+import functools
 import math
 import jax
 import jax.numpy as jnp
@@ -13,6 +14,20 @@
 CFL = 0.04
 DTC = 0.2
 PRECISE = lax.Precision.HIGHEST
+
+
+def cycles_switch(base_x, dim_at):
+    long_array = lax.all_to_all(
+        jnp.stack(tuple((base_x for _ in range(lax.axis_size("modes")))), 0),
+        axis_name="modes",
+        split_axis=0,
+        concat_axis=0,
+    )
+    field_out = jnp.concatenate(long_array, dim_at)
+    return field_out
+
+
+put_cells = functools.partial(cycles_switch, dim_at=0)
 
 
 def passed_along(shard, axis, by):
@@ -141,7 +156,7 @@
         quadratic_factors, encounter_kernel_array, preferred_element_type=jnp.float32
     )
     lifted = jnp.dot(
-        lax.all_gather(scattered_state, "modes", axis=0, tiled=True),
+        put_cells(scattered_state),
         selector.T,
         precision=PRECISE,
         preferred_element_type=jnp.float32,

time: 488 us -> 444 us (0.910)
  waiting for transfers between devices: 343 us -> 260 us
  blocking collectives: 0 us -> 40.4 us
    all_gather x1 -> x0, waiting for transfers between devices: 83.6 us -> none  [body(): lax.all_gather(scattered_state, 'modes', axis=0, tiled=True)]
    all_to_all x0 -> x1, blocking collectives: none -> 40.4 us  [cycles_switch(): lax.all_to_all(jnp.stack(tuple((base_x for _ in range(lax.axis_size('mode...]
  transfers between devices with their start and end apart: 10 -> 9, of which waited for: 7 -> 6; matrix products, arithmetic and copies ran while one was open for 2% -> 2% of each run, Pallas kernels for 0% -> 0%
where the time goes in v1:
time: 444 us; the launch traced here: 443 us
  waiting for transfers between devices  260 us (59%)
  starting transfers between devices  74.7 us (17%)
  blocking collectives  40.4 us (9%)
  matrix products  25.7 us (6%)
  local copies, waits for them, and re-layouts  15.3 us (3%)
  between operations  13.8 us (3%)
  other arithmetic  13.3 us (3%)
    reduce_scatter x1, waiting for transfers between devices, body(): lax.psum_scatter(jnp.dot(rows, selector, precision=PRECISE, preferred_ele...  149 us
    ppermute x4, waiting for transfers between devices, passed_along(): return lax.ppermute(shard, axis, pairs)  87.8 us
    ppermute x2, starting transfers between devices, extended(): lax.ppermute(tail, axis, [(i, (i + 1) % count) for i in range(count)])  59.8 us
    all_to_all x1, blocking collectives, cycles_switch(): lax.all_to_all(jnp.stack(tuple((base_x for _ in range(lax.axis_size('mode...  40.4 us
    dot_general x2, matrix products, substep(): jnp.dot(jnp.concatenate([first_axis_gradient, diff_y, diff_z], -1), full_...  18.8 us
    ppermute x4, starting transfers between devices, passed_along(): return lax.ppermute(shard, axis, pairs)  13.2 us
    ppermute x2, waiting for transfers between devices, extended(): lax.ppermute(tail, axis, [(i, (i + 1) % count) for i in range(count)])  13.1 us
    ppermute x2, waiting for transfers between devices, extended(): lax.ppermute(head, axis, [((i + 1) % count, i) for i in range(count)])  10 us
  transfers between devices with their start and end apart: 9, of which 6 were waited for; matrix products, arithmetic and copies ran while one was open for 2% of the time, Pallas kernels for 0%

profile of v1, /device:TPU:6, one launch (start us, length us, event | category | flops | bytes accessed | tf_op | source)
XLA Modules:
  0.0 443.4 jit_solution(12569997891433344468)
XLA Ops:
  6.5 3.2 fusion.65
  9.7 1.7 collective-permute-start
  11.8 12.5 %collective-permute-done.1 = f32[1,64,32,128]{3,2,1,0:T(8,128)} collective-permute-done((f32[1,64,32,128]{3,2,1,0:T(8,128)}, f32[1,64,32,128]{3,2,1,0:T(8,128)}, u32[]{:S(2)}, u32[]{:S(2)}) %collective-permute-start.1) | collective-permute-done | bytes 1048608 | tf_op jit(solution)/shard_map/ppermute | solution.py:46
  24.3 2.7 fusion.23
  26.9 1.3 collective-permute-start.3
  28.2 4.7 %collective-permute-start.2 = (f32[2,64,32,128]{3,2,1,0:T(8,128)S(1)}, f32[2,64,32,128]{3,2,1,0:T(8,128)S(1)}, u32[]{:S(2)}, u32[]{:S(2)}) collective-permute-start(f32[2,64,32,128]{3,2,1,0:T(8,128)S(1)} %fusion.23), channel_id=1, source_target_pairs={{0,1},{1,2},{2,3},{3,4},{4,5},{5,6},{6,7},{7,8},{8,9},{9,10},{10,1... | collective-permute-start | bytes 6291464 | tf_op jit(solution)/shard_map/ppermute | solution.py:36
  36.3 35.1 %collective-permute-done.3 = f32[2,64,32,128]{3,2,1,0:T(8,128)S(1)} collective-permute-done((f32[2,64,32,128]{3,2,1,0:T(8,128)S(1)}, f32[2,64,32,128]{3,2,1,0:T(8,128)S(1)}, u32[]{:S(2)}, u32[]{:S(2)}) %collective-permute-start.3) | collective-permute-done | bytes 2097184 | tf_op jit(solution)/shard_map/ppermute | solution.py:36
  71.4 1.3 copy-done.9
  73.5 9.4 %add_select_fusion.1 = f32[2,64,32,128]{3,2,1,0:T(8,128)S(1)} fusion(f32[2,64,32,128]{3,2,1,0:T(8,128)S(1)} %copy-done.1, f32[2,64,32,128]{3,2,1,0:T(8,128)} %copy-done.9, f32[2,64,32,128]{3,2,1,0:T(8,128)} %copy-done.10, f32[2,63,32,128]{3,2,1,0:T(8,128)S(1)} %get-tuple-element.20, f32[2,1,32,128]{3,2,1,0:T(8,128)S(1)} %get-tuple-element.22, ...), kind=kOutput, calls=%fused_computation.16 | convolution fusion | flops 2433318912 | bytes 25366536 | tf_op jit(solution)/shard_map/dot_general | solution.py:117
  82.9 1.6 fusion.60
  84.9 59.8 %collective-permute-start.5 = (f32[1,64,32,128]{3,2,1,0:T(8,128)}, f32[1,64,32,128]{3,2,1,0:T(8,128)}, u32[]{:S(2)}, u32[]{:S(2)}) collective-permute-start(f32[1,64,32,128]{3,2,1,0:T(8,128)} %get-tuple-element.13), channel_id=1, source_target_pairs={{0,16},{16,32},{32,48},{48,64},{64,80},{80,96},{96,112},{112,128},... | collective-permute-start | bytes 3145736 | tf_op jit(solution)/shard_map/ppermute | solution.py:46
  147.3 10.0 %collective-permute-done.4 = f32[1,64,32,128]{3,2,1,0:T(8,128)} collective-permute-done((f32[1,64,32,128]{3,2,1,0:T(8,128)}, f32[1,64,32,128]{3,2,1,0:T(8,128)}, u32[]{:S(2)}, u32[]{:S(2)}) %collective-permute-start.4) | collective-permute-done | bytes 1048608 | tf_op jit(solution)/shard_map/ppermute | solution.py:48
  157.3 2.6 fusion.24
  161.3 5.9 %collective-permute-start.6 = (f32[2,64,32,128]{3,2,1,0:T(8,128)S(1)}, f32[2,64,32,128]{3,2,1,0:T(8,128)}, u32[]{:S(2)}, u32[]{:S(2)}) collective-permute-start(f32[2,64,32,128]{3,2,1,0:T(8,128)S(1)} %fusion.24), channel_id=1, source_target_pairs={{0,1},{1,2},{2,3},{3,4},{4,5},{5,6},{6,7},{7,8},{8,9},{9,10},{10,1... | collective-permute-start | bytes 6291464 | tf_op jit(solution)/shard_map/ppermute | solution.py:36
  169.8 52.6 %collective-permute-done.7 = f32[2,64,32,128]{3,2,1,0:T(8,128)S(1)} collective-permute-done((f32[2,64,32,128]{3,2,1,0:T(8,128)S(1)}, f32[2,64,32,128]{3,2,1,0:T(8,128)S(1)}, u32[]{:S(2)}, u32[]{:S(2)}) %collective-permute-start.7) | collective-permute-done | bytes 2097184 | tf_op jit(solution)/shard_map/ppermute | solution.py:36
  222.4 1.3 copy-done.11
  223.7 9.4 %add_select_fusion = f32[2,64,32,128]{3,2,1,0:T(8,128)S(1)} fusion(f32[2,64,32,128]{3,2,1,0:T(8,128)S(1)} %copy-done.3, f32[2,64,32,128]{3,2,1,0:T(8,128)} %copy-done.11, f32[2,64,32,128]{3,2,1,0:T(8,128)} %collective-permute-done.6, f32[2,63,32,128]{3,2,1,0:T(8,128)S(1)} %get-tuple-element.10, f32[2,1,32,128]{3,2,1,0:T(8,128)S(1)} %get-tuple-element.12, ...), kind=kOutput, calls=%fused_computation.15 | convolution fusion | flops 2433318912 | bytes 25366536 | tf_op jit(solution)/shard_map/dot_general | solution.py:117
  233.1 1.3 copy-done.4
  234.4 2.5 fusion.27
  237.0 149.4 %reduce-scatter.2.cloned.1.call-done = f32[256,120]{0,1:T(8,128)} async-done(((f32[4096,120]{0,1:T(8,128)}), f32[256,120]{0,1:T(8,128)}) %reduce-scatter.2.cloned.1.call-update) | async-done | bytes 122896 | tf_op jit(solution)/shard_map/reduce_scatter | solution.py:144
  386.4 3.7 multiply_convert_fusion
  391.4 40.4 %all_to_all.5 = f32[16,256,120]{1,2,0:T(8,128)S(1)} all-to-all(f32[16,256,120]{1,2,0:T(8,128)S(1)} %stack.2), channel_id=1, replica_groups=mesh['cells'=16,'modes'=16] {'modes'}, dimensions={0} | all-to-all | bytes 3932160 | tf_op jit(solution)/shard_map/all_to_all | solution.py:20
  431.9 1.4 copy-done.5
  433.3 3.2 fusion.12
  (67 shorter events, 12.5 us)
Async XLA Ops:
  6.5 383.6 %copy-start = (bf16[14400,120]{0,1:T(8,128)(2,1)S(1)}, bf16[14400,120]{0,1:T(8,128)(2,1)}, u32[]{:S(2)}) copy-start(bf16[14400,120]{0,1:T(8,128)(2,1)} %param.4) | copy-start | bytes 10368004
  6.5 5.0 %copy-start.6 = (s32[2,64,32]{1,2,0:T(8,128)S(1)}, s32[2,64,32]{1,2,0:T(8,128)}, u32[]{:S(2)}) copy-start(s32[2,64,32]{1,2,0:T(8,128)} %param.5) | copy-start | bytes 49156
  6.5 379.8 %reduce-scatter.2.cloned.1.call-start = ((), (), s32[]{:S(2)}) async-start(), calls=%async_computation.2 | async-start | bytes 2088960 | tf_op jit(solution)/shard_map/reduce_scatter | solution.py:144
  9.7 14.5 %collective-permute-start.1 = (f32[1,64,32,128]{3,2,1,0:T(8,128)}, f32[1,64,32,128]{3,2,1,0:T(8,128)}, u32[]{:S(2)}, u32[]{:S(2)}) collective-permute-start(f32[1,64,32,128]{3,2,1,0:T(8,128)} %get-tuple-element.23), channel_id=1, source_target_pairs={{0,16},{16,32},{32,48},{48,64},{64,80},{80,96},{96,112},{112,128},... | collective-permute-start | bytes 3145736 | tf_op jit(solution)/shard_map/ppermute | solution.py:46
  9.7 14.5 %collective-permute-start = (f32[1,64,32,128]{3,2,1,0:T(8,128)}, f32[1,64,32,128]{3,2,1,0:T(8,128)}, u32[]{:S(2)}, u32[]{:S(2)}) collective-permute-start(f32[1,64,32,128]{3,2,1,0:T(8,128)} %get-tuple-element.24), channel_id=1, source_target_pairs={{16,0},{32,16},{48,32},{64,48},{80,64},{96,80},{112,96},{128,112},... | collective-permute-start | bytes 3145736 | tf_op jit(solution)/shard_map/ppermute | solution.py:48
  11.7 61.8 %copy-start.7 = (pred[2,64,32]{2,1,0:T(8,128)(4,1)}, pred[2,64,32]{2,1,0:T(8,128)(4,1)S(1)}, u32[]{:S(2)}) copy-start(pred[2,64,32]{2,1,0:T(8,128)(4,1)S(1)} %copy.11) | copy-start | bytes 12292
  11.8 21.2 %copy-start.1 = (f32[2,64,32,128]{3,2,1,0:T(8,128)S(1)}, f32[2,64,32,128]{3,2,1,0:T(8,128)}, u32[]{:S(2)}) copy-start(f32[2,64,32,128]{3,2,1,0:T(8,128)} %param.3) | copy-start | bytes 6291460
  26.9 44.5 %collective-permute-start.3 = (f32[2,64,32,128]{3,2,1,0:T(8,128)S(1)}, f32[2,64,32,128]{3,2,1,0:T(8,128)S(1)}, u32[]{:S(2)}, u32[]{:S(2)}) collective-permute-start(f32[2,64,32,128]{3,2,1,0:T(8,128)S(1)} %fusion.23), channel_id=1, source_target_pairs={{1,0},{2,1},{3,2},{4,3},{5,4},{6,5},{7,6},{8,7},{9,8},{10,9},{11,1... | collective-permute-start | bytes 6291464 | tf_op jit(solution)/shard_map/ppermute | solution.py:36
  28.2 43.2 %collective-permute-start.2 = (f32[2,64,32,128]{3,2,1,0:T(8,128)S(1)}, f32[2,64,32,128]{3,2,1,0:T(8,128)S(1)}, u32[]{:S(2)}, u32[]{:S(2)}) collective-permute-start(f32[2,64,32,128]{3,2,1,0:T(8,128)S(1)} %fusion.23), channel_id=1, source_target_pairs={{0,1},{1,2},{2,3},{3,4},{4,5},{5,6},{6,7},{7,8},{8,9},{9,10},{10,1... | collective-permute-start | bytes 6291464 | tf_op jit(solution)/shard_map/ppermute | solution.py:36
  71.4 1.3 copy-start.9
  71.4 2.0 copy-start.10
  82.9 2.0 copy-start.2
  84.9 62.4 %collective-permute-start.5 = (f32[1,64,32,128]{3,2,1,0:T(8,128)}, f32[1,64,32,128]{3,2,1,0:T(8,128)}, u32[]{:S(2)}, u32[]{:S(2)}) collective-permute-start(f32[1,64,32,128]{3,2,1,0:T(8,128)} %get-tuple-element.13), channel_id=1, source_target_pairs={{0,16},{16,32},{32,48},{48,64},{64,80},{80,96},{96,112},{112,128},... | collective-permute-start | bytes 3145736 | tf_op jit(solution)/shard_map/ppermute | solution.py:46
  144.7 12.6 %collective-permute-start.4 = (f32[1,64,32,128]{3,2,1,0:T(8,128)}, f32[1,64,32,128]{3,2,1,0:T(8,128)}, u32[]{:S(2)}, u32[]{:S(2)}) collective-permute-start(f32[1,64,32,128]{3,2,1,0:T(8,128)} %get-tuple-element.14), channel_id=1, source_target_pairs={{16,0},{32,16},{48,32},{64,48},{80,64},{96,80},{112,96},{128,112},... | collective-permute-start | bytes 3145736 | tf_op jit(solution)/shard_map/ppermute | solution.py:48
  146.7 20.7 %copy-start.3 = (f32[2,64,32,128]{3,2,1,0:T(8,128)S(1)}, f32[2,64,32,128]{3,2,1,0:T(8,128)}, u32[]{:S(2)}) copy-start(f32[2,64,32,128]{3,2,1,0:T(8,128)} %copy-done.2) | copy-start | bytes 6291460
  160.0 62.4 %collective-permute-start.7 = (f32[2,64,32,128]{3,2,1,0:T(8,128)S(1)}, f32[2,64,32,128]{3,2,1,0:T(8,128)S(1)}, u32[]{:S(2)}, u32[]{:S(2)}) collective-permute-start(f32[2,64,32,128]{3,2,1,0:T(8,128)S(1)} %fusion.24), channel_id=1, source_target_pairs={{1,0},{2,1},{3,2},{4,3},{5,4},{6,5},{7,6},{8,7},{9,8},{10,9},{11,1... | collective-permute-start | bytes 6291464 | tf_op jit(solution)/shard_map/ppermute | solution.py:36
  161.3 62.4 %collective-permute-start.6 = (f32[2,64,32,128]{3,2,1,0:T(8,128)S(1)}, f32[2,64,32,128]{3,2,1,0:T(8,128)}, u32[]{:S(2)}, u32[]{:S(2)}) collective-permute-start(f32[2,64,32,128]{3,2,1,0:T(8,128)S(1)} %fusion.24), channel_id=1, source_target_pairs={{0,1},{1,2},{2,3},{3,4},{4,5},{5,6},{6,7},{7,8},{8,9},{9,10},{10,1... | collective-permute-start | bytes 6291464 | tf_op jit(solution)/shard_map/ppermute | solution.py:36
  169.2 54.5 %copy-start.8 = (pred[2,64,32]{2,1,0:T(8,128)(4,1)S(1)}, pred[2,64,32]{2,1,0:T(8,128)(4,1)}, u32[]{:S(2)}) copy-start(pred[2,64,32]{2,1,0:T(8,128)(4,1)} %copy-done.7) | copy-start | bytes 12292
  222.4 1.3 copy-start.11
  233.1 1.3 copy-start.4
  431.7 1.6 copy-start.5
Sparse Core Ops, SparseCore 0:
  237.1 149.2 reduce-scatter.1
